TPU v7x, 32 devices: a whole 2x2x4 slice. The times are simulated.
32 devices in a mesh: parts: 2 (over y), row: 4 (over z), col: 4 (over x, core).
Axes of the slice: x: 2, y: 2, z: 4, core: 2. Of those that a mesh axis runs over, the one named last changes fastest.
Arguments:
- amplitudes: bfloat16 [8, 100, 512, 512], P('parts', 'col', 'row'), parts along dimension 0, may hold values from -12 to 12
- integrals: bfloat16 [200, 512, 512], P(('parts', 'col'), 'row'), parts along dimension 0, may hold values from -0.109375 to 0.109375
- occ_irrep: int32 [200], P('parts'), parts along dimension 0, may hold values from 0 to 7, as said below
- vir_irrep: int32 [1024], P('parts'), parts along dimension 0, may hold values from 0 to 7, as said below
- screen: int32 [200, 8], P('parts'), parts along dimension 0, may hold values 0 or 1
- occ_energy: float32 [200], P('parts'), parts along dimension 0, may hold values from -1 to -0.3
- vir_energy: float32 [1024], P('parts'), parts along dimension 0, may hold values from 0.1 to 1
Outputs:
- update: float32 [512, 8, 512], P('row', 'parts', 'col'), parts along dimension 1
There are 2 independent parts, one for each index of `parts`. A program takes and returns all parts, laid end to end along the dimension named above; each array names one. Nothing has to cross between parts.
Inputs may be any that keep to these rules, and one draw needn't show every extreme that they name: `occ_irrep`: the labels never fall from one orbital to the next; the first is 0 and the last is 7. `vir_irrep`: the labels never fall from one orbital to the next and every label from 0 to 7 occurs; exactly one label covers 256 virtual orbitals, every other label fewer.
All inputs are finite; a program needn't handle non-finite values.
Results may differ from a plain program's by a relative error of at most 0.0003.
Values may be sent and summed in bfloat16 or wider, within the bound.
A program may use at most 128 MiB of HBM per device.

v0:
```python
import jax
import jax.numpy as jnp
from jax import lax
from jax.sharding import PartitionSpec as P


def folded_integrals(integrals, occ_local, vir_local, vir_irrep, screen_rows, pair_label):
    half = vir_irrep.shape[0] // 2
    irrep_codes = jnp.arange(8, dtype=jnp.int32)
    screen_local = jnp.sum(
        screen_rows[:, None, :] * (vir_local[None, :, None] == irrep_codes).astype(jnp.int32),
        axis=2,
    )
    wanted = jnp.bitwise_xor(jnp.bitwise_xor(occ_local[:, None], vir_local[None, :]), pair_label)
    wanted = jnp.where(screen_local == 1, wanted, -1)[:, :, None]
    zeros = jnp.zeros((), integrals.dtype)
    low = jnp.where(wanted == vir_irrep[None, None, :half], integrals[:, :, :half], zeros)
    return jnp.where(wanted == vir_irrep[None, None, half:], integrals[:, :, half:], low)


def on_device(amplitudes, integrals, occ_irrep, vir_irrep, screen, occ_energy, vir_energy):
    row_count = lax.axis_size("row")
    column_count = lax.axis_size("col")
    row, col = (lax.axis_index("row"), lax.axis_index("col"))
    batch_size, occ_share, vir_share, vir_total = amplitudes.shape
    half = vir_total // 2
    vir_columns = vir_total // column_count
    occ_offset = col * occ_share
    occ_local = lax.dynamic_slice_in_dim(occ_irrep, occ_offset, occ_share)
    vir_local = lax.dynamic_slice_in_dim(vir_irrep, row * vir_share, vir_share)
    screen_rows = lax.dynamic_slice_in_dim(screen, occ_offset, occ_share, 0)
    pair_label = occ_irrep[batch_size]
    folded = folded_integrals(integrals, occ_local, vir_local, vir_irrep, screen_rows, pair_label)
    gathered = lax.all_gather(folded, "row", axis=1, tiled=True)
    shift = jnp.bitwise_xor(occ_irrep[:batch_size, None], occ_local[None, :])
    keep_amp = (
        jnp.bitwise_xor(shift[:, :, None], vir_local[None, None, :])[:, :, :, None]
        == vir_irrep[None, None, None, :]
    )
    amp_kept = jnp.where(keep_amp, amplitudes, jnp.zeros_like(amplitudes))
    partial = lax.dot_general(
        amp_kept, gathered, (((1, 3), (0, 1)), ((), ())), preferred_element_type=jnp.float32
    )
    if row_count == column_count and column_count == 4:
        piece = lax.psum_scatter(partial, "col", scatter_dimension=2, tiled=True)
        routes = []
        for flip in (0, 1):
            pairs = []
            for r in range(row_count):
                for q in range(column_count):
                    target = q // 2 + 2 * ((q + flip) % 2)
                    pairs.append((r * column_count + q, target * column_count + r))
            routes.append(lax.ppermute(piece, ("row", "col"), pairs))
        swap = row // 2 == 1
        first = jnp.where(swap, routes[1], routes[0])
        second = jnp.where(swap, routes[0], routes[1])
        cycle = jnp.concatenate([first, second], axis=2)
    else:
        whole = lax.all_gather(lax.psum(partial, "col"), "row", axis=1, tiled=True)
        cycle = lax.dynamic_slice_in_dim(whole, col * vir_columns, vir_columns, 1)
        cycle = lax.dynamic_slice_in_dim(cycle, row * vir_share % half, vir_share, 2)
    cycle = jnp.transpose(cycle, (2, 0, 1))
    col_irrep = lax.dynamic_slice_in_dim(vir_irrep, col * vir_columns, vir_columns)
    kept = (
        jnp.bitwise_xor(occ_irrep[:batch_size, None], pair_label ^ col_irrep[None, :])[None]
        == vir_local[:, None, None]
    )
    cycle = jnp.where(kept, cycle, 0.0)
    energy_cols = lax.dynamic_slice_in_dim(vir_energy, col * vir_columns, vir_columns)
    energy_rows = lax.dynamic_slice_in_dim(vir_energy, row * vir_share, vir_share)
    denominator = (
        occ_energy[:batch_size][None, :, None]
        + occ_energy[batch_size]
        - energy_cols[None, None, :]
        - energy_rows[:, None, None]
    )
    return cycle / denominator


def solution(mesh):
    in_specs = (
        P("parts", "col", "row", None),
        P(("parts", "col"), "row", None),
        P("parts"),
        P("parts"),
        P("parts", None),
        P("parts"),
        P("parts"),
    )
    out_specs = P("row", "parts", "col")
    return jax.shard_map(
        on_device, mesh=mesh, in_specs=in_specs, out_specs=out_specs, check_vma=False
    )
```

profile of v0, /device:TPU:2, one launch (start us, length us, event | category | flops | bytes accessed | tf_op | source)
XLA Modules:
  0.0 192.5 jit_solution(17666716235107848208)
XLA Ops:
  6.5 1.2 slice.26
  7.8 0.8 fusion.14
  8.5 1.5 dynamic-slice_xor_fusion
  10.0 0.7 dynamic_slice.20
  10.8 0.1 constant_dynamic-slice_fusion
  10.8 0.1 copy.12
  10.9 3.4 %fusion.12 = (bf16[25,128,256]{2,1,0:T(8,128)(2,1)}, bf16[25,128,256]{2,1,0:T(8,128)(2,1)S(1)}) fusion(bf16[25,128,512]{2,1,0:T(8,128)(2,1)} %param.8), kind=kLoop, calls=%fused_computation.26 | loop fusion | bytes 6553600 | tf_op jit(solution)/shard_map/slice | solution.py:17
  14.4 2.1 %copy.17 = bf16[25,128,256]{1,2,0:T(8,128)(2,1)S(1)} copy(bf16[25,128,256]{2,1,0:T(8,128)(2,1)S(1)} %get-tuple-element.6) | data formatting | bytes 3276800
  16.5 3.1 %copy.18 = bf16[25,128,256]{1,2,0:T(8,128)(2,1)S(1)} copy(bf16[25,128,256]{2,1,0:T(8,128)(2,1)} %get-tuple-element.5) | data formatting | bytes 3276800
  19.6 0.1 multiply_reduce_fusion
  19.7 0.7 xor_select_fusion
  20.4 2.1 %compare_select_fusion.3 = bf16[25,128,256]{1,2,0:T(8,128)(2,1)} fusion(bf16[25,128,256]{1,2,0:T(8,128)(2,1)S(1)} %copy.17, bf16[25,128,256]{1,2,0:T(8,128)(2,1)S(1)} %copy.18, s32[25,128]{1,0:T(8,128)S(1)} %xor_select_fusion, s32[256]{0:T(256)S(1)} %get-tuple-element.14, s32[256]{0:T(256)S(1)} %get-tuple-element.13), kind=kLoop, calls=%fused_computation.7 | loop fusion | flops 3276800 | bytes 4930048 | tf_op jit(solution)/shard_map/jit(_where)/select_n | solution.py:18
  22.5 0.0 all-gather.2.cloned.1.call-update
  22.5 0.0 reduce-scatter.2.cloned.1.call-start
  22.6 0.1 broadcast_xor_fusion.1
  22.6 0.1 broadcast_xor_fusion
  22.7 10.7 %compare_select_fusion.8 = bf16[4,25,128,512]{3,2,1,0:T(8,128)(2,1)} fusion(bf16[4,25,128,512]{3,2,1,0:T(8,128)(2,1)} %param.7, s32[512]{0:T(512)S(1)} %copy-done.1, s32[4,25,128]{2,1,0:T(8,128)S(1)} %broadcast_xor_fusion), kind=kLoop, calls=%fused_computation.clone.clone.clone.clone.1 | loop fusion | flops 13107200 | bytes 26267648 | tf_op jit(solution)/shard_map/dot_general | solution.py:41
  33.4 109.6 %all-gather.2.cloned.1.call-done = bf16[25,512,256]{1,2,0:T(8,128)(2,1)} async-done(((bf16[25,128,256]{1,2,0:T(8,128)(2,1)}), bf16[25,512,256]{1,2,0:T(8,128)(2,1)}) %all-gather.2.cloned.1.call-update) | async-done | bytes 6553616 | tf_op jit(solution)/shard_map/all_gather | solution.py:34
  143.0 9.2 %fusion.5 = f32[4,128,256]{1,2,0:T(8,128)} fusion(bf16[25,512,256]{1,2,0:T(8,128)(2,1)} %all-gather.2.cloned.1.call-done, bf16[4,25,128,512]{3,2,1,0:T(8,128)(2,1)} %compare_select_fusion.8), kind=kOutput, calls=%fused_computation.8 | convolution fusion | flops 3355443200 | bytes 20185088 | tf_op jit(solution)/shard_map/dot_general | solution.py:41
  152.2 0.0 reduce-scatter.2.cloned.1.call-update
  152.3 0.6 slice.32
  152.9 0.1 fusion.13
  153.0 0.6 slice_add_fusion
  153.6 0.1 broadcast_xor_fusion.2
  153.7 17.4 %reduce-scatter.2.cloned.1.call-done = f32[4,128,64]{1,2,0:T(8,128)} async-done(((f32[4,128,256]{1,2,0:T(8,128)}), f32[4,128,64]{1,2,0:T(8,128)}) %reduce-scatter.2.cloned.1.call-update) | async-done | bytes 131088 | tf_op jit(solution)/shard_map/reduce_scatter | solution.py:45
  171.1 4.5 %collective-permute-start = (f32[4,128,64]{1,2,0:T(8,128)}, f32[4,128,64]{1,2,0:T(8,128)S(1)}, u32[]{:S(2)}, u32[]{:S(2)}) collective-permute-start(f32[4,128,64]{1,2,0:T(8,128)} %reduce-scatter.2.cloned.1.call-done), channel_id=1, source_target_pairs={{0,8},{1,0},{2,12},{3,4},{4,9},{5,1},{6,13},{7,5},{8,10},{9,2},{10... | collective-permute-start | bytes 393224 | tf_op jit(solution)/shard_map/ppermute | solution.py:53
  175.6 1.9 collective-permute-start.1
  177.5 0.1 broadcast_subtract_fusion
  177.6 1.5 collective-permute-done
  179.0 5.6 %collective-permute-done.1 = f32[4,128,64]{1,2,0:T(8,128)S(1)} collective-permute-done((f32[4,128,64]{1,2,0:T(8,128)}, f32[4,128,64]{1,2,0:T(8,128)S(1)}, u32[]{:S(2)}, u32[]{:S(2)}) %collective-permute-start.1) | collective-permute-done | bytes 131104 | tf_op jit(solution)/shard_map/ppermute | solution.py:53
  184.7 0.1 fusion.9
  184.8 0.9 copy.15
  (13 shorter events, 0.0 us)
Async XLA Ops:
  6.5 4.2 %copy-start = (s32[100,8]{0,1:T(8,128)S(1)}, s32[100,8]{0,1:T(8,128)}, u32[]{:S(2)}) copy-start(s32[100,8]{0,1:T(8,128)} %param.11) | copy-start | bytes 9604
  6.5 136.5 %all-gather.2.cloned.1.call-start = ((), (), s32[]{:S(2)}) async-start(), calls=%async_computation.1 | async-start | bytes 8192000 | tf_op jit(solution)/shard_map/all_gather | solution.py:34
  20.4 2.1 %copy-start.2 = (s32[100]{0:T(128)S(1)}, s32[100]{0:T(128)}, u32[]{:S(2)}) copy-start(s32[100]{0:T(128)} %param.9) | copy-start | bytes 1204
  20.4 2.3 %copy-start.1 = (s32[512]{0:T(512)S(1)}, s32[512]{0:T(512)}, u32[]{:S(2)}) copy-start(s32[512]{0:T(512)} %param.10) | copy-start | bytes 6148
  22.5 148.6 %reduce-scatter.2.cloned.1.call-start = ((), (), s32[]{:S(2)}) async-start(), calls=%async_computation.2 | async-start | bytes 655360 | tf_op jit(solution)/shard_map/reduce_scatter | solution.py:45
  33.4 118.8 %copy-start.4 = (f32[100]{0:T(128)S(1)}, f32[100]{0:T(128)}, u32[]{:S(2)}) copy-start(f32[100]{0:T(128)} %param.12) | copy-start | bytes 1204
  33.4 119.4 %copy-start.3 = (f32[512]{0:T(512)S(1)}, f32[512]{0:T(512)}, u32[]{:S(2)}) copy-start(f32[512]{0:T(512)} %param.13) | copy-start | bytes 6148
  171.1 7.9 %collective-permute-start = (f32[4,128,64]{1,2,0:T(8,128)}, f32[4,128,64]{1,2,0:T(8,128)S(1)}, u32[]{:S(2)}, u32[]{:S(2)}) collective-permute-start(f32[4,128,64]{1,2,0:T(8,128)} %reduce-scatter.2.cloned.1.call-done), channel_id=1, source_target_pairs={{0,8},{1,0},{2,12},{3,4},{4,9},{5,1},{6,13},{7,5},{8,10},{9,2},{10... | collective-permute-start | bytes 393224 | tf_op jit(solution)/shard_map/ppermute | solution.py:53
  175.6 9.0 %collective-permute-start.1 = (f32[4,128,64]{1,2,0:T(8,128)}, f32[4,128,64]{1,2,0:T(8,128)S(1)}, u32[]{:S(2)}, u32[]{:S(2)}) collective-permute-start(f32[4,128,64]{1,2,0:T(8,128)} %reduce-scatter.2.cloned.1.call-done), channel_id=1, source_target_pairs={{0,0},{1,8},{2,4},{3,12},{4,1},{5,9},{6,5},{7,13},{8,2},{9,10},{10... | collective-permute-start | bytes 393224 | tf_op jit(solution)/shard_map/ppermute | solution.py:53
Sparse Core Ops, SparseCore 0:
  22.6 120.3 all-gather.1
  152.4 18.6 reduce-scatter.1
where the time goes:
time: 193 us; the launch traced here: 192 us
  waiting for transfers between devices  134 us (69%)
  other arithmetic  16.1 us (8%)
  between operations  13.5 us (7%)
  local copies, waits for them, and re-layouts  13.1 us (7%)
  matrix products  9.22 us (5%)
  starting transfers between devices  6.42 us (3%)
    all_gather x1, waiting for transfers between devices, on_device(): gathered = lax.all_gather(folded, 'row', axis=1, tiled=True)  110 us
    reduce_scatter x1, waiting for transfers between devices, on_device(): piece = lax.psum_scatter(partial, 'col', scatter_dimension=2, tiled=True)  17.4 us
    dot_general x1, other arithmetic, on_device(): lax.dot_general(amp_kept, gathered, (((1, 3), (0, 1)), ((), ())), preferr...  10.7 us
    dot_general x1, matrix products, on_device(): lax.dot_general(amp_kept, gathered, (((1, 3), (0, 1)), ((), ())), preferr...  9.22 us
    ppermute x2, waiting for transfers between devices, on_device(): routes.append(lax.ppermute(piece, ('row', 'col'), pairs))  7.05 us
    ppermute x2, starting transfers between devices, on_device(): routes.append(lax.ppermute(piece, ('row', 'col'), pairs))  6.37 us
    unnamed x12, local copies, waits for them, and re-layouts  5.25 us
  transfers between devices with their start and end apart: 4, of which 4 were waited for; matrix products, arithmetic and copies ran while one was open for 6% of the time, Pallas kernels for 0%

commit v1 on v0

--- a/solution.py
+++ b/solution.py
@@ -2,6 +2,18 @@
 import jax.numpy as jnp
 from jax import lax
 from jax.sharding import PartitionSpec as P
+
+
+def collect(array, axis, dim):
+    ways, here, lap = (lax.axis_size(axis), lax.axis_index(axis), array.shape[dim])
+    lengths = [n * ways if d == dim else n for d, n in enumerate(array.shape)]
+    full = lax.dynamic_update_slice_in_dim(
+        jnp.zeros(lengths, array.dtype), array, here * lap, axis=dim
+    )
+    for far in range(1, ways):
+        array = lax.ppermute(array, axis, [(d, (d + 1) % ways) for d in range(ways)])
+        full = lax.dynamic_update_slice_in_dim(full, array, (here - far) % ways * lap, axis=dim)
+    return full
 
 
 def folded_integrals(integrals, occ_local, vir_local, vir_irrep, screen_rows, pair_label):
@@ -31,7 +43,7 @@
     screen_rows = lax.dynamic_slice_in_dim(screen, occ_offset, occ_share, 0)
     pair_label = occ_irrep[batch_size]
     folded = folded_integrals(integrals, occ_local, vir_local, vir_irrep, screen_rows, pair_label)
-    gathered = lax.all_gather(folded, "row", axis=1, tiled=True)
+    gathered = collect(folded, "row", 1)
     shift = jnp.bitwise_xor(occ_irrep[:batch_size, None], occ_local[None, :])
     keep_amp = (
         jnp.bitwise_xor(shift[:, :, None], vir_local[None, None, :])[:, :, :, None]

time: 193 us -> 184 us (0.953)
  waiting for transfers between devices: 134 us -> 116 us
  local copies, waits for them, and re-layouts: 13.1 us -> 20.1 us
    all_gather x1 -> x0, waiting for transfers between devices: 110 us -> none  [on_device(): gathered = lax.all_gather(folded, 'row', axis=1, tiled=True)]
    ppermute x0 -> x3, waiting for transfers between devices: none -> 91.5 us  [collect(): lax.ppermute(array, axis, [(d, (d + 1) % ways) for d in range(ways)])]
    ppermute x0 -> x3, local copies, waits for them, and re-layouts: none -> 8.34 us  [collect(): lax.ppermute(array, axis, [(d, (d + 1) % ways) for d in range(ways)])]
    unnamed x12, local copies, waits for them, and re-layouts: 5.25 us -> 0.03 us
    dynamic_update_slice x0 -> x4, local copies, waits for them, and re-layouts: none -> 4.45 us  [the longest x3 4.06 us: collect(): lax.dynamic_update_slice_in_dim(full, array, (here - far) % ways * lap, a...]
    slice x1 -> x0, local copies, waits for them, and re-layouts: 3.42 us -> none  [folded_integrals(): integrals[:, :, :half]]
    select_n x0 -> x1, local copies, waits for them, and re-layouts: none -> 2.11 us  [folded_integrals(): jnp.where(wanted == vir_irrep[None, None, half:], integrals[:, :, half:],...]
  transfers between devices with their start and end apart: 4 -> 6, of which waited for: 4 -> 6; matrix products, arithmetic and copies ran while one was open for 6% -> 13% of each run, Pallas kernels for 0% -> 0%
where the time goes in v1:
time: 184 us; the launch traced here: 183 us
  waiting for transfers between devices  116 us (63%)
  local copies, waits for them, and re-layouts  20.1 us (11%)
  other arithmetic  16.4 us (9%)
  between operations  13.6 us (7%)
  matrix products  9.24 us (5%)
  starting transfers between devices  8.01 us (4%)
    ppermute x3, waiting for transfers between devices, collect(): lax.ppermute(array, axis, [(d, (d + 1) % ways) for d in range(ways)])  91.5 us
    reduce_scatter x1, waiting for transfers between devices, on_device(): piece = lax.psum_scatter(partial, 'col', scatter_dimension=2, tiled=True)  17.4 us
    dot_general x1, other arithmetic, on_device(): lax.dot_general(amp_kept, gathered, (((1, 3), (0, 1)), ((), ())), preferr...  10.6 us
    dot_general x1, matrix products, on_device(): lax.dot_general(amp_kept, gathered, (((1, 3), (0, 1)), ((), ())), preferr...  9.24 us
    ppermute x3, local copies, waits for them, and re-layouts, collect(): lax.ppermute(array, axis, [(d, (d + 1) % ways) for d in range(ways)])  8.34 us
    ppermute x2, waiting for transfers between devices, on_device(): routes.append(lax.ppermute(piece, ('row', 'col'), pairs))  7.07 us
    ppermute x2, starting transfers between devices, on_device(): routes.append(lax.ppermute(piece, ('row', 'col'), pairs))  6.38 us
    dynamic_update_slice x3, local copies, waits for them, and re-layouts, collect(): lax.dynamic_update_slice_in_dim(full, array, (here - far) % ways * lap, a...  4.06 us
  transfers between devices with their start and end apart: 6, of which 6 were waited for; matrix products, arithmetic and copies ran while one was open for 13% of the time, Pallas kernels for 0%

profile of v1, /device:TPU:2, one launch (start us, length us, event | category | flops | bytes accessed | tf_op | source)
XLA Modules:
  0.0 183.4 jit_solution(9004910136406322872)
XLA Ops:
  6.5 1.2 slice.26
  7.8 0.8 fusion.13
  8.5 1.5 dynamic-slice_xor_fusion
  10.0 0.7 dynamic_slice.20
  10.8 0.1 copy.14
  10.9 0.1 multiply_reduce_fusion
  11.0 0.7 xor_select_fusion
  11.8 2.4 %compare_select_fusion.3 = bf16[25,128,256]{2,1,0:T(8,128)(2,1)S(1)} fusion(bf16[25,128,512]{2,1,0:T(8,128)(2,1)} %param.8, s32[256]{0:T(256)S(1)} %get-tuple-element.12, s32[256]{0:T(256)S(1)} %get-tuple-element.11, s32[25,128]{1,0:T(8,128)S(1)} %xor_select_fusion), kind=kLoop, calls=%fused_computation.7 | loop fusion | flops 3276800 | bytes 4930048 | tf_op jit(solution)/shard_map/jit(_where)/select_n | solution.py:30
  14.2 1.6 collective-permute-start
  15.9 37.9 %collective-permute-done = bf16[25,128,256]{2,1,0:T(8,128)(2,1)} collective-permute-done((bf16[25,128,256]{2,1,0:T(8,128)(2,1)S(1)}, bf16[25,128,256]{2,1,0:T(8,128)(2,1)}, u32[]{:S(2)}, u32[]{:S(2)}) %collective-permute-start) | collective-permute-done | bytes 1638432 | tf_op jit(solution)/shard_map/ppermute | solution.py:14
  53.8 2.1 %copy.15 = bf16[25,128,256]{1,2,0:T(8,128)(2,1)S(1)} copy(bf16[25,128,256]{2,1,0:T(8,128)(2,1)S(1)} %compare_select_fusion.3) | data formatting | bytes 3276800 | tf_op jit(solution)/shard_map/jit(_where)/select_n | solution.py:30
  56.0 0.7 broadcast_in_dim.16
  56.7 0.4 constant_dynamic-update-slice_fusion.3
  57.3 35.4 %collective-permute-done.1 = bf16[25,128,256]{2,1,0:T(8,128)(2,1)} collective-permute-done((bf16[25,128,256]{2,1,0:T(8,128)(2,1)}, bf16[25,128,256]{2,1,0:T(8,128)(2,1)}, u32[]{:S(2)}, u32[]{:S(2)}) %collective-permute-start.1) | collective-permute-done | bytes 1638432 | tf_op jit(solution)/shard_map/ppermute | solution.py:14
  92.6 10.6 %compare_select_fusion.8 = bf16[4,25,128,512]{3,2,1,0:T(8,128)(2,1)} fusion(bf16[4,25,128,512]{3,2,1,0:T(8,128)(2,1)} %param.7, s32[512]{0:T(512)S(1)} %copy-done.2, s32[4,25,128]{2,1,0:T(8,128)S(1)} %broadcast_xor_fusion), kind=kLoop, calls=%fused_computation.clone.clone.clone.clone.1 | loop fusion | flops 13107200 | bytes 26267648 | tf_op jit(solution)/shard_map/dot_general | solution.py:53
  103.2 3.1 %copy.16 = bf16[25,128,256]{1,2,0:T(8,128)(2,1)S(1)} copy(bf16[25,128,256]{2,1,0:T(8,128)(2,1)} %collective-permute-done) | data formatting | bytes 3276800 | tf_op jit(solution)/shard_map/ppermute | solution.py:14
  106.4 1.4 constant_dynamic-update-slice_fusion.2
  107.8 3.1 %copy.17 = bf16[25,128,256]{1,2,0:T(8,128)(2,1)S(1)} copy(bf16[25,128,256]{2,1,0:T(8,128)(2,1)} %collective-permute-done.1) | data formatting | bytes 3276800 | tf_op jit(solution)/shard_map/ppermute | solution.py:14
  110.9 1.3 constant_dynamic-update-slice_fusion.1
  112.2 18.2 %collective-permute-done.2 = bf16[25,128,256]{2,1,0:T(8,128)(2,1)S(1)} collective-permute-done((bf16[25,128,256]{2,1,0:T(8,128)(2,1)}, bf16[25,128,256]{2,1,0:T(8,128)(2,1)S(1)}, u32[]{:S(2)}, u32[]{:S(2)}) %collective-permute-start.2) | collective-permute-done | bytes 1638432 | tf_op jit(solution)/shard_map/ppermute | solution.py:14
  130.5 2.1 %copy.18 = bf16[25,128,256]{1,2,0:T(8,128)(2,1)S(1)} copy(bf16[25,128,256]{2,1,0:T(8,128)(2,1)S(1)} %collective-permute-done.2) | data formatting | bytes 3276800 | tf_op jit(solution)/shard_map/ppermute | solution.py:14
  132.6 1.3 constant_dynamic-update-slice_fusion
  133.9 9.2 %fusion.5 = f32[4,128,256]{1,2,0:T(8,128)} fusion(bf16[25,512,256]{1,2,0:T(8,128)(2,1)} %constant_dynamic-update-slice_fusion, bf16[4,25,128,512]{3,2,1,0:T(8,128)(2,1)} %compare_select_fusion.8), kind=kOutput, calls=%fused_computation.8 | convolution fusion | flops 3355443200 | bytes 20185088 | tf_op jit(solution)/shard_map/dot_general | solution.py:53
  143.2 0.6 slice.32
  143.9 0.6 slice_add_fusion
  144.6 17.4 %reduce-scatter.2.cloned.1.call-done = f32[4,128,64]{1,2,0:T(8,128)} async-done(((f32[4,128,256]{1,2,0:T(8,128)}), f32[4,128,64]{1,2,0:T(8,128)}) %reduce-scatter.2.cloned.1.call-update) | async-done | bytes 131088 | tf_op jit(solution)/shard_map/reduce_scatter | solution.py:57
  162.0 4.5 %collective-permute-start.3 = (f32[4,128,64]{1,2,0:T(8,128)}, f32[4,128,64]{1,2,0:T(8,128)S(1)}, u32[]{:S(2)}, u32[]{:S(2)}) collective-permute-start(f32[4,128,64]{1,2,0:T(8,128)} %reduce-scatter.2.cloned.1.call-done), channel_id=1, source_target_pairs={{0,8},{1,0},{2,12},{3,4},{4,9},{5,1},{6,13},{7,5},{8,10},{9,2},{10... | collective-permute-start | bytes 393224 | tf_op jit(solution)/shard_map/ppermute | solution.py:65
  166.5 1.9 %collective-permute-start.4 = (f32[4,128,64]{1,2,0:T(8,128)}, f32[4,128,64]{1,2,0:T(8,128)S(1)}, u32[]{:S(2)}, u32[]{:S(2)}) collective-permute-start(f32[4,128,64]{1,2,0:T(8,128)} %reduce-scatter.2.cloned.1.call-done), channel_id=1, source_target_pairs={{0,0},{1,8},{2,4},{3,12},{4,1},{5,9},{6,5},{7,13},{8,2},{9,10},{10... | collective-permute-start | bytes 393224 | tf_op jit(solution)/shard_map/ppermute | solution.py:65
  168.5 1.5 collective-permute-done.3
  169.9 5.6 %collective-permute-done.4 = f32[4,128,64]{1,2,0:T(8,128)S(1)} collective-permute-done((f32[4,128,64]{1,2,0:T(8,128)}, f32[4,128,64]{1,2,0:T(8,128)S(1)}, u32[]{:S(2)}, u32[]{:S(2)}) %collective-permute-start.4) | collective-permute-done | bytes 131104 | tf_op jit(solution)/shard_map/ppermute | solution.py:65
  175.6 0.1 fusion.9
  175.7 0.9 copy.19
  (24 shorter events, 0.5 us)
Async XLA Ops:
  6.5 4.2 %copy-start = (s32[100,8]{0,1:T(8,128)S(1)}, s32[100,8]{0,1:T(8,128)}, u32[]{:S(2)}) copy-start(s32[100,8]{0,1:T(8,128)} %param.11) | copy-start | bytes 9604
  6.5 155.5 %reduce-scatter.2.cloned.1.call-start = ((), (), s32[]{:S(2)}) async-start(), calls=%async_computation.1 | async-start | bytes 655360 | tf_op jit(solution)/shard_map/reduce_scatter | solution.py:57
  14.2 42.9 %copy-start.3 = (s32[100]{0:T(128)S(1)}, s32[100]{0:T(128)}, u32[]{:S(2)}) copy-start(s32[100]{0:T(128)} %param.9) | copy-start | bytes 1204
  14.2 78.4 %copy-start.2 = (s32[512]{0:T(512)S(1)}, s32[512]{0:T(512)}, u32[]{:S(2)}) copy-start(s32[512]{0:T(512)} %param.10) | copy-start | bytes 6148
  14.2 39.6 %collective-permute-start = (bf16[25,128,256]{2,1,0:T(8,128)(2,1)S(1)}, bf16[25,128,256]{2,1,0:T(8,128)(2,1)}, u32[]{:S(2)}, u32[]{:S(2)}) collective-permute-start(bf16[25,128,256]{2,1,0:T(8,128)(2,1)S(1)} %compare_select_fusion.3), channel_id=1, source_target_pairs={{0,4},{4,8},{8,12},{12,0},{1,5},{5,9},{9,13},{13,1},{2,6},{6,10},{... | collective-permute-start | bytes 4915208 | tf_op jit(solution)/shard_map/ppermute | solution.py:14
  53.8 38.9 %collective-permute-start.1 = (bf16[25,128,256]{2,1,0:T(8,128)(2,1)}, bf16[25,128,256]{2,1,0:T(8,128)(2,1)}, u32[]{:S(2)}, u32[]{:S(2)}) collective-permute-start(bf16[25,128,256]{2,1,0:T(8,128)(2,1)} %collective-permute-done), channel_id=1, source_target_pairs={{0,4},{4,8},{8,12},{12,0},{1,5},{5,9},{9,13},{13,1},{2,6},{6,10},{... | collective-permute-start | bytes 4915208 | tf_op jit(solution)/shard_map/ppermute | solution.py:14
  57.1 35.5 %copy-start.1 = (bf16[25,512,256]{1,2,0:T(8,128)(2,1)}, bf16[25,512,256]{1,2,0:T(8,128)(2,1)S(1)}, u32[]{:S(2)}) copy-start(bf16[25,512,256]{1,2,0:T(8,128)(2,1)S(1)} %constant_dynamic-update-slice_fusion.3) | copy-start | bytes 19660804
  92.6 37.8 %collective-permute-start.2 = (bf16[25,128,256]{2,1,0:T(8,128)(2,1)}, bf16[25,128,256]{2,1,0:T(8,128)(2,1)S(1)}, u32[]{:S(2)}, u32[]{:S(2)}) collective-permute-start(bf16[25,128,256]{2,1,0:T(8,128)(2,1)} %collective-permute-done.1), channel_id=1, source_target_pairs={{0,4},{4,8},{8,12},{12,0},{1,5},{5,9},{9,13},{13,1},{2,6},{6,10},{... | collective-permute-start | bytes 4915208 | tf_op jit(solution)/shard_map/ppermute | solution.py:14
  133.9 9.3 %copy-start.5 = (f32[100]{0:T(128)S(1)}, f32[100]{0:T(128)}, u32[]{:S(2)}) copy-start(f32[100]{0:T(128)} %param.12) | copy-start | bytes 1204
  133.9 9.9 %copy-start.4 = (f32[512]{0:T(512)S(1)}, f32[512]{0:T(512)}, u32[]{:S(2)}) copy-start(f32[512]{0:T(512)} %param.13) | copy-start | bytes 6148
  162.0 7.9 %collective-permute-start.3 = (f32[4,128,64]{1,2,0:T(8,128)}, f32[4,128,64]{1,2,0:T(8,128)S(1)}, u32[]{:S(2)}, u32[]{:S(2)}) collective-permute-start(f32[4,128,64]{1,2,0:T(8,128)} %reduce-scatter.2.cloned.1.call-done), channel_id=1, source_target_pairs={{0,8},{1,0},{2,12},{3,4},{4,9},{5,1},{6,13},{7,5},{8,10},{9,2},{10... | collective-permute-start | bytes 393224 | tf_op jit(solution)/shard_map/ppermute | solution.py:65
  166.5 9.1 %collective-permute-start.4 = (f32[4,128,64]{1,2,0:T(8,128)}, f32[4,128,64]{1,2,0:T(8,128)S(1)}, u32[]{:S(2)}, u32[]{:S(2)}) collective-permute-start(f32[4,128,64]{1,2,0:T(8,128)} %reduce-scatter.2.cloned.1.call-done), channel_id=1, source_target_pairs={{0,0},{1,8},{2,4},{3,12},{4,1},{5,9},{6,5},{7,13},{8,2},{9,10},{10... | collective-permute-start | bytes 393224 | tf_op jit(solution)/shard_map/ppermute | solution.py:65
Sparse Core Ops, SparseCore 0:
  143.3 18.6 reduce-scatter.1
